TPU v7x, 1024 devices: a whole 4x8x16 slice. The times are simulated.
1024 devices in a mesh: row: 4 (over x_lo, core), mesh: 256 (over y, z, x_hi).
Axes of the slice: x: 4 (x_hi: 2, x_lo: 2; x = x_hi * 2 + x_lo), y: 8, z: 16, core: 2. Of those that a mesh axis runs over, the one named last changes fastest.
Arguments:
- state: float32 [4, 7, 5, 8192, 256], P('row', None, None, 'mesh'), may hold values from -6 to 6
- inverse_blocks: float32 [4, 5, 5, 8192, 256], P('row', None, None, 'mesh'), may hold values from -0.25 to 0.5
- flux_jacobian: float32 [4, 5, 5], P('row'), may hold values from -2.5 to 2.5
- harmonics: int32 [4, 3], replicated, may hold values from 1 to 17, as said below
- interface_delay: float32 [4], replicated, may hold values from 0 to 1
- inflow: float32 [7, 5, 8192], P(None, None, 'mesh'), may hold values from -6 to 6
- pairing: int32 [4, 8192], P('row', 'mesh'), may hold values from 0 to 8191, as said below
Outputs:
- updated: float32 [4, 7, 5, 8192, 256], P('row', None, None, 'mesh')
Inputs may be any that keep to these rules, and one draw needn't show every extreme that they name: `harmonics`: each row's harmonic numbers leave the remainders 1 to 3 in some order when divided by 7. `pairing`: within each aligned block of 32 lines, a permutation of that block's lines.
All inputs are finite; a program needn't handle non-finite values.
Results may differ from a plain program's by a relative error of at most 0.00016.
Values sent between devices are 32-bit elements; how exact they have to be, the bound alone decides.
No kernel may reach another device: no remote copies, remote signals or barrier semaphores. Data moves between devices by JAX's collectives and lax.ppermute only.
A program may use at most 32 MiB of HBM per device.

v0:
```python
import jax
import jax.numpy as jnp
from jax import lax
from jax.sharding import PartitionSpec as P

TIME_SAMPLES = 7
SECTIONS = 3


largest_mode = lax.Precision.HIGHEST
nu_second = 0.25
nu_fourth = 0.03
time_scale = 0.05


def from_behind(array, axis, by):
    devices = lax.axis_size(axis)
    pairs = [(i, i + by) for i in range(devices) if 0 <= i + by < devices]
    return lax.ppermute(array, axis, pairs)


def padded_2(array, sides, width):
    for axis, dim in sides:
        devices, length = (lax.axis_size(axis), array.shape[dim])
        up = [(i, (i + 1) % devices) for i in range(devices - 1)]
        down = [(j, i) for i, j in up]
        last = lax.slice_in_dim(array, length - width, length, axis=dim)
        first = lax.slice_in_dim(array, 0, width, axis=dim)
        before = lax.ppermute(last, axis, up)
        after = lax.ppermute(first, axis, down)
        array = jnp.concatenate([before, array, after], axis=dim)
    return array


def spectral_basis(sample_times, harmonic_modes):
    phase_angles = (
        2.0 * jnp.pi * sample_times[:, None] * harmonic_modes[None, :].astype(jnp.float32)
    )
    column_of_ones = jnp.ones((sample_times.shape[0], 1), jnp.float32)
    return jnp.concatenate([column_of_ones, jnp.cos(phase_angles), jnp.sin(phase_angles)], axis=1)


def basis_derivative(sample_times, harmonic_modes):
    angular_speeds = 2.0 * jnp.pi * harmonic_modes.astype(jnp.float32)
    phase_angles = sample_times[:, None] * angular_speeds[None, :]
    column_of_zeros = jnp.zeros((sample_times.shape[0], 1), jnp.float32)
    return jnp.concatenate(
        [
            column_of_zeros,
            -angular_speeds[None, :] * jnp.sin(phase_angles),
            angular_speeds[None, :] * jnp.cos(phase_angles),
        ],
        axis=1,
    )


def forward_transform(sample_times, harmonic_modes):
    sample_count = sample_times.shape[0]
    mode_weights = jnp.concatenate(
        [
            jnp.full((1,), 1.0 / sample_count, jnp.float32),
            jnp.full((sample_count - 1,), 2.0 / sample_count, jnp.float32),
        ]
    )
    return mode_weights[:, None] * spectral_basis(sample_times, harmonic_modes).T


def row_operators(harmonics, interface_delay, blade_row_index):
    sample_times = jnp.arange(TIME_SAMPLES, dtype=jnp.float32) / TIME_SAMPLES
    local_modes = harmonics[blade_row_index]
    upstream_modes = harmonics[jnp.maximum(blade_row_index - 1, 0)]
    spectral_derivative = jnp.dot(
        basis_derivative(sample_times, local_modes),
        forward_transform(sample_times, local_modes),
        precision=largest_mode,
        preferred_element_type=jnp.float32,
    )
    interface_mapping = jnp.dot(
        spectral_basis(sample_times + interface_delay[blade_row_index], upstream_modes),
        forward_transform(sample_times, upstream_modes),
        precision=largest_mode,
        preferred_element_type=jnp.float32,
    )
    return (spectral_derivative, interface_mapping)


def section_residual(padded, ghost_cells, spectral_derivative, flux_jac):
    centre = padded[:, :, 2:-2]
    before = jnp.concatenate([ghost_cells[:, :, :, None], centre[:, :, :, :-1]], axis=3)
    advection = jnp.einsum("ab,tbwl->tawl", flux_jac, centre - before, precision=largest_mode)
    second_diff = padded[:, :, 3:-1] - 2.0 * centre + padded[:, :, 1:-3]
    fourth_diff = (
        padded[:, :, 4:]
        - 4.0 * padded[:, :, 3:-1]
        + 6.0 * centre
        - 4.0 * padded[:, :, 1:-3]
        + padded[:, :, :-4]
    )
    temporal = jnp.einsum("ts,svwl->tvwl", spectral_derivative, centre, precision=largest_mode)
    return advection - nu_second * second_diff + nu_fourth * fourth_diff + time_scale * temporal


def apply_block(inverse, residual):
    total = inverse[None, :, 0] * residual[:, 0][:, None]
    for column_index in range(1, inverse.shape[1]):
        total = total + inverse[None, :, column_index] * residual[:, column_index][:, None]
    return total


def body(state, inverse_blocks, flux_jacobian, harmonics, interface_delay, inflow, pairing):
    blade_row_index = lax.axis_index("row")
    spectral_derivative, interface_mapping = row_operators(
        harmonics, interface_delay, blade_row_index
    )
    local_state = state[0]
    local_inverse = inverse_blocks[0]
    flux_jac = flux_jacobian[0]
    sample_count, variable_count, line_count, cell_count = local_state.shape
    outlet = local_state[:, :, :, -1]
    received = from_behind(outlet, "row", 1)
    upstream = jnp.where(blade_row_index == 0, inflow, received)
    local_pairs = pairing[0] - lax.axis_index("mesh") * line_count
    paired = jnp.take(upstream, local_pairs, axis=2)
    ghost_cells = jnp.einsum("ts,svw->tvw", interface_mapping, paired, precision=largest_mode)
    current = local_state
    for section_index in range(SECTIONS):
        padded = padded_2(current, (("mesh", 2),), 2)
        residual = section_residual(padded, ghost_cells, spectral_derivative, flux_jac)
        section_weight = (section_index + 1.0) / SECTIONS
        current = local_state - section_weight * apply_block(local_inverse, residual)
    return current[None]


def solution(mesh):
    return jax.shard_map(
        body,
        mesh=mesh,
        in_specs=(
            P("row", None, None, "mesh", None),
            P("row", None, None, "mesh", None),
            P("row", None, None),
            P(),
            P(),
            P(None, None, "mesh"),
            P("row", "mesh"),
        ),
        out_specs=P("row", None, None, "mesh", None),
        check_vma=False,
    )
```

profile of v0, /device:TPU:33, one launch (start us, length us, event | category | flops | bytes accessed | tf_op | source)
XLA Modules:
  0.0 116.4 jit_solution(5772249774567772907)
XLA Ops:
  0.0 1.9 %copy.150 = f32[1,7,5,32,256]{4,2,3,1,0:T(8,128)S(1)} copy(f32[1,7,5,32,256]{4,3,2,1,0:T(8,128)} %param.7) | data formatting | bytes 2293760 | tf_op args[0]
  1.9 0.7 fusion.136
  2.7 20.3 %collective-permute-start.1 = (f32[7,5,2,256]{3,1,2,0:T(8,128)}, f32[7,5,2,256]{3,1,2,0:T(8,128)}, u32[]{:S(2)}, u32[]{:S(2)}) collective-permute-start(f32[7,5,2,256]{3,1,2,0:T(8,128)} %get-tuple-element.24), channel_id=1, source_target_pairs={{1,0},{2,1},{3,2},{4,3},{5,4},{6,5},{7,6},{8,7},{9,8},{10,9},{11,1... | collective-permute-start | bytes 215048 | tf_op jit(solution)/shard_map/ppermute | solution.py:30
  22.9 1.9 %collective-permute-start.2 = (f32[7,5,2,256]{3,1,2,0:T(8,128)}, f32[7,5,2,256]{3,1,2,0:T(8,128)}, u32[]{:S(2)}, u32[]{:S(2)}) collective-permute-start(f32[7,5,2,256]{3,1,2,0:T(8,128)} %get-tuple-element.25), channel_id=1, source_target_pairs={{0,1},{1,2},{2,3},{3,4},{4,5},{5,6},{6,7},{7,8},{8,9},{9,10},{10,1... | collective-permute-start | bytes 215048 | tf_op jit(solution)/shard_map/ppermute | solution.py:29
  24.9 0.3 slice.199
  25.2 2.3 %copy.66 = f32[7,5,32,1]{1,0,2,3:T(8,128)} copy(f32[7,5,32,1]{3,1,2,0:T(8,128)S(1)} %slice.199) | data formatting | bytes 8960 | tf_op jit(solution)/shard_map/squeeze | solution.py:119
  27.4 3.0 %collective-permute-start = (f32[7,5,32]{1,0,2:T(8,128)}, f32[7,5,32]{1,0,2:T(8,128)}, u32[]{:S(2)}, u32[]{:S(2)}) collective-permute-start(f32[7,5,32]{1,0,2:T(8,128)} %bitcast.8), channel_id=1, source_target_pairs={{0,256},{256,512},{512,768},{1,257},{257,513},{513,769},{2,258},{2... | collective-permute-start | bytes 13448 | tf_op jit(solution)/shard_map/ppermute | solution.py:19
  30.5 0.5 compare_and_fusion
  31.1 1.4 %slice_bitcast_fusion.2 = f32[1,7,5,32,255]{4,2,3,1,0:T(8,128)} fusion(f32[7,5,32,256]{3,1,2,0:T(8,128)S(1)} %bitcast.143), kind=kLoop, calls=%fused_computation.64 | loop fusion | bytes 2284800 | tf_op jit(solution)/shard_map/concatenate | solution.py:89
  32.5 0.6 dynamic_slice.9
  33.1 0.7 iota_multiply_fusion
  33.8 2.1 %slice_bitcast_fusion.7 = (f32[5,32,256]{2,1,0:T(8,128)S(1)}, f32[5,32,256]{2,1,0:T(8,128)}, f32[5,32,256]{2,1,0:T(8,128)}, f32[5,32,256]{2,1,0:T(8,128)}, f32[5,32,256]{2,1,0:T(8,128)}) fusion(f32[5,5,32,256]{3,2,1,0:T(8,128)} %bitcast.170), kind=kLoop, calls=%fused_computation.146 | loop fusion | bytes 1638400 | tf_op jit(solution)/shard_map/mul | solution.py:104
  35.9 0.1 fusion.95
  36.0 0.1 multiply_cosine_fusion.2
  36.2 0.2 convolution_bitcast_fusion.1
  36.4 2.9 %fusion.63 = f32[7,5,32,256]{3,0,2,1:T(8,128)} fusion(f32[7,7,1,1]{1,0,3,2:T(8,128)S(1)} %convolution_bitcast_fusion.1, f32[7,5,32,256]{3,2,1,0:T(8,128)S(1)} %bitcast.140), kind=kOutput, calls=%fused_computation.96 | convolution fusion | flops 24084480 | bytes 2293956 | tf_op jit(solution)/shard_map/ts,svwl->tvwl/dot_general | solution.py:99
  39.3 0.2 convolution_bitcast_fusion.2
  39.5 0.8 copy.39
  40.4 1.0 copy.48
  41.4 1.7 %copy.47 = f32[5,32,256]{2,0,1:T(8,128)} copy(f32[5,32,256]{2,1,0:T(8,128)} %get-tuple-element.28) | data formatting | bytes 327680 | tf_op jit(solution)/shard_map/mul | solution.py:106
  43.1 1.7 %copy.46 = f32[5,32,256]{2,0,1:T(8,128)} copy(f32[5,32,256]{2,1,0:T(8,128)} %get-tuple-element.29) | data formatting | bytes 327680 | tf_op jit(solution)/shard_map/mul | solution.py:106
  44.9 1.7 %copy.45 = f32[5,32,256]{2,0,1:T(8,128)} copy(f32[5,32,256]{2,1,0:T(8,128)} %get-tuple-element.30) | data formatting | bytes 327680 | tf_op jit(solution)/shard_map/mul | solution.py:106
  46.6 1.6 %broadcast_select_fusion = f32[7,5,32]{1,0,2:T(8,128)} fusion(f32[7,5,32]{1,0,2:T(8,128)S(1)} %copy-done.5, f32[7,5,32]{1,0,2:T(8,128)} %collective-permute-done, pred[]{:T(512)S(6)} %eq.3), kind=kLoop, calls=%fused_computation.148 | loop fusion | flops 1120 | bytes 13441 | tf_op jit(solution)/shard_map/jit(_where)/select_n | solution.py:121
  48.2 2.1 %gather_fusion = f32[32,7,5]{2,1,0:T(8,128)} fusion(f32[7,5,32]{1,0,2:T(8,128)} %broadcast_select_fusion, s32[1024]{0:T(1024)S(1)} %pad_clamp_fusion), kind=kCustom, calls=%fused_computation | custom fusion | bytes 9088 | tf_op jit(solution)/shard_map/jit(_take)/gather | solution.py:123
  50.3 1.7 %select_bitcast_fusion = f32[7,5,32]{1,0,2:T(8,128)} fusion(f32[32,7,5]{2,1,0:T(8,128)} %gather_fusion, pred[32]{0:T(512)(128)(4,1)S(1)} %copy-done.9), kind=kLoop, calls=%fused_computation.147 | loop fusion | flops 1120 | bytes 8992 | tf_op jit(solution)/shard_map/jit(_take)/select_n | solution.py:123
  51.9 1.0 copy.40
  53.0 0.2 convolution_bitcast_fusion
  53.1 1.3 %copy.41 = f32[1,7,5,32,1]{4,2,3,1,0:T(8,128)} copy(f32[1,7,5,32,1]{3,1,2,4,0:T(8,128)S(1)} %convolution_bitcast_fusion) | data formatting | bytes 8960 | tf_op jit(solution)/shard_map/concatenate | solution.py:89
  54.4 5.9 %fusion.34 = f32[7,5,32,256]{3,1,2,0:T(8,128)S(1)} fusion(f32[7,5,32,256]{3,1,2,0:T(8,128)S(1)} %bitcast.144, f32[7,5,2,256]{3,1,2,0:T(8,128)} %collective-permute-done.2, f32[7,5,2,256]{3,1,2,0:T(8,128)} %collective-permute-done.1, f32[7,5,32,256]{3,0,2,1:T(8,128)} %fusion.63, f32[1,7,5,32,1]{4,2,3,1,0:T(8,128)} %copy.41, ...), kind=kOutput, calls=%fused_computation.59 | convolution fusion | flops 23511040 | bytes 5877860 | tf_op jit(solution)/shard_map/ab,tbwl->tawl/dot_general | solution.py:90
  60.4 1.0 fusion.135
  61.6 1.6 %multiply_subtract_fusion.1 = f32[7,5,32,256]{3,1,2,0:T(8,128)S(1)} fusion(f32[7,32,256]{2,1,0:T(8,128)S(1)} %bitcast.153, f32[5,32,256]{2,0,1:T(8,128)S(1)} %copy.48, f32[7,32,256]{2,1,0:T(8,128)S(1)} %bitcast.157, f32[5,32,256]{2,0,1:T(8,128)S(1)} %copy-done.1, f32[7,32,256]{2,1,0:T(8,128)S(1)} %bitcast.159, f32[5,32,256]{2,0,1:T(8,128)S(1)} %copy-done.2, ...), kind=kLoop, calls=%fused_computation.85 | loop fusion | flops 3153920 | bytes 4259840 | tf_op jit(solution)/shard_map/sub | solution.py:130
  63.3 0.2 slice_bitcast_fusion.1
  63.5 10.1 %collective-permute-start.3 = (f32[7,5,2,256]{3,1,2,0:T(8,128)S(1)}, f32[7,5,2,256]{3,1,2,0:T(8,128)S(1)}, u32[]{:S(2)}, u32[]{:S(2)}) collective-permute-start(f32[7,5,2,256]{3,1,2,0:T(8,128)S(1)} %get-tuple-element.17), channel_id=1, source_target_pairs={{1,0},{2,1},{3,2},{4,3},{5,4},{6,5},{7,6},{8,7},{9,8},{10,9},{11,1... | collective-permute-start | bytes 215048 | tf_op jit(solution)/shard_map/ppermute | solution.py:30
  73.6 2.1 %collective-permute-start.4 = (f32[7,5,2,256]{3,1,2,0:T(8,128)S(1)}, f32[7,5,2,256]{3,1,2,0:T(8,128)S(1)}, u32[]{:S(2)}, u32[]{:S(2)}) collective-permute-start(f32[7,5,2,256]{3,1,2,0:T(8,128)S(1)} %get-tuple-element.18), channel_id=1, source_target_pairs={{0,1},{1,2},{2,3},{3,4},{4,5},{5,6},{6,7},{7,8},{8,9},{9,10},{10,1... | collective-permute-start | bytes 215048 | tf_op jit(solution)/shard_map/ppermute | solution.py:29
  75.7 1.8 %fusion.67 = f32[7,5,32,256]{3,0,2,1:T(8,128)S(1)} fusion(f32[7,7,1,1]{1,0,3,2:T(8,128)S(1)} %convolution_bitcast_fusion.1, f32[7,5,32,256]{3,1,2,0:T(8,128)S(1)} %multiply_subtract_fusion.1), kind=kOutput, calls=%fused_computation.100 | convolution fusion | flops 24084480 | bytes 2293956 | tf_op jit(solution)/shard_map/ts,svwl->tvwl/dot_general | solution.py:99
  77.5 7.6 %collective-permute-done.4 = f32[7,5,2,256]{3,1,2,0:T(8,128)S(1)} collective-permute-done((f32[7,5,2,256]{3,1,2,0:T(8,128)S(1)}, f32[7,5,2,256]{3,1,2,0:T(8,128)S(1)}, u32[]{:S(2)}, u32[]{:S(2)}) %collective-permute-start.4) | collective-permute-done | bytes 71712 | tf_op jit(solution)/shard_map/ppermute | solution.py:29
  85.1 4.8 %fusion.27 = f32[7,5,32,256]{3,1,2,0:T(8,128)S(1)} fusion(f32[7,5,32,256]{3,1,2,0:T(8,128)S(1)} %multiply_subtract_fusion.1, f32[7,5,2,256]{3,1,2,0:T(8,128)S(1)} %collective-permute-done.4, f32[7,5,2,256]{3,1,2,0:T(8,128)S(1)} %collective-permute-done.3, f32[7,5,32,256]{3,0,2,1:T(8,128)S(1)} %fusion.67, f32[1,7,5,32,1]{4,2,3,1,0:T(8,128)S(1)} %copy-done.4, ...), kind=kOutput, calls=%fused_computation.49 | convolution fusion | flops 26664960 | bytes 7843940 | tf_op jit(solution)/shard_map/ab,tbwl->tawl/dot_general | solution.py:90
  89.9 1.0 fusion.133
  91.1 1.6 %multiply_subtract_fusion = f32[7,5,32,256]{3,1,2,0:T(8,128)S(1)} fusion(f32[7,32,256]{2,1,0:T(8,128)S(1)} %bitcast.147, f32[7,32,256]{2,1,0:T(8,128)S(1)} %bitcast.151, f32[7,32,256]{2,1,0:T(8,128)S(1)} %bitcast.155, f32[7,32,256]{2,1,0:T(8,128)S(1)} %bitcast.161, f32[7,32,256]{2,1,0:T(8,128)S(1)} %bitcast.145, f32[5,32,256]{2,0,1:T(8,128)S(1)} %copy.48, ...), kind=kLoop, calls=%fused_computation.74 | loop fusion | flops 3153920 | bytes 4259840 | tf_op jit(solution)/shard_map/sub | solution.py:130
  92.8 0.2 slice_bitcast_fusion
  93.0 1.9 %collective-permute-start.5 = (f32[7,5,2,256]{3,1,2,0:T(8,128)S(1)}, f32[7,5,2,256]{3,1,2,0:T(8,128)S(1)}, u32[]{:S(2)}, u32[]{:S(2)}) collective-permute-start(f32[7,5,2,256]{3,1,2,0:T(8,128)S(1)} %get-tuple-element.10), channel_id=1, source_target_pairs={{1,0},{2,1},{3,2},{4,3},{5,4},{6,5},{7,6},{8,7},{9,8},{10,9},{11,1... | collective-permute-start | bytes 215048 | tf_op jit(solution)/shard_map/ppermute | solution.py:30
  94.9 5.1 %collective-permute-start.6 = (f32[7,5,2,256]{3,1,2,0:T(8,128)S(1)}, f32[7,5,2,256]{3,1,2,0:T(8,128)S(1)}, u32[]{:S(2)}, u32[]{:S(2)}) collective-permute-start(f32[7,5,2,256]{3,1,2,0:T(8,128)S(1)} %get-tuple-element.11), channel_id=1, source_target_pairs={{0,1},{1,2},{2,3},{3,4},{4,5},{5,6},{6,7},{7,8},{8,9},{9,10},{10,1... | collective-permute-start | bytes 215048 | tf_op jit(solution)/shard_map/ppermute | solution.py:29
  100.0 1.8 %fusion.65 = f32[7,5,32,256]{3,0,2,1:T(8,128)S(1)} fusion(f32[7,7,1,1]{1,0,3,2:T(8,128)S(1)} %convolution_bitcast_fusion.1, f32[7,5,32,256]{3,1,2,0:T(8,128)S(1)} %multiply_subtract_fusion), kind=kOutput, calls=%fused_computation.98 | convolution fusion | flops 24084480 | bytes 2293956 | tf_op jit(solution)/shard_map/ts,svwl->tvwl/dot_general | solution.py:99
  101.8 5.7 %collective-permute-done.6 = f32[7,5,2,256]{3,1,2,0:T(8,128)S(1)} collective-permute-done((f32[7,5,2,256]{3,1,2,0:T(8,128)S(1)}, f32[7,5,2,256]{3,1,2,0:T(8,128)S(1)}, u32[]{:S(2)}, u32[]{:S(2)}) %collective-permute-start.6) | collective-permute-done | bytes 71712 | tf_op jit(solution)/shard_map/ppermute | solution.py:29
  107.5 4.8 %fusion.20 = f32[7,5,32,256]{3,1,2,0:T(8,128)S(1)} fusion(f32[7,5,32,256]{3,1,2,0:T(8,128)S(1)} %multiply_subtract_fusion, f32[7,5,2,256]{3,1,2,0:T(8,128)S(1)} %collective-permute-done.6, f32[7,5,2,256]{3,1,2,0:T(8,128)S(1)} %collective-permute-done.5, f32[7,5,32,256]{3,0,2,1:T(8,128)S(1)} %fusion.65, f32[1,7,5,32,1]{4,2,3,1,0:T(8,128)S(1)} %copy-done.4, ...), kind=kOutput, calls=%fused_computation.39 | convolution fusion | flops 26664960 | bytes 7843940 | tf_op jit(solution)/shard_map/ab,tbwl->tawl/dot_general | solution.py:90
  112.3 1.0 fusion.131
  113.4 1.6 %copy_subtract_fusion.3 = f32[1,7,5,32,256]{4,2,3,1,0:T(8,128)S(1)} fusion(f32[1,7,5,32,256]{4,3,2,1,0:T(8,128)S(1)} %copy-done, f32[7,32,256]{2,1,0:T(8,128)S(1)} %bitcast.166, f32[7,32,256]{2,1,0:T(8,128)S(1)} %bitcast.167, f32[7,32,256]{2,1,0:T(8,128)S(1)} %bitcast.168, f32[7,32,256]{2,1,0:T(8,128)S(1)} %bitcast.169, f32[7,32,256]{2,1,0:T(8,128)S(1)} %bitcast.165, ...), kind=kLoop, calls=%fused_computation.5 | loop fusion | flops 2867200 | bytes 4259840 | tf_op jit(solution)/shard_map/sub | solution.py:130
  115.0 1.3 %copy.63 = f32[1,7,5,32,256]{4,3,2,1,0:T(8,128)} copy(f32[1,7,5,32,256]{4,2,3,1,0:T(8,128)S(1)} %copy_subtract_fusion.3) | data formatting | bytes 2293760 | tf_op jit(solution)/shard_map/sub | solution.py:130
  (56 shorter events, 0.5 us)
Async XLA Ops:
  1.9 28.6 %copy-start.11 = (s32[1,32]{1,0:T(1,128)S(1)}, s32[1,32]{1,0:T(1,128)}, u32[]{:S(2)}) copy-start(s32[1,32]{1,0:T(1,128)} %param.13) | copy-start | bytes 388
  2.7 51.8 %collective-permute-start.1 = (f32[7,5,2,256]{3,1,2,0:T(8,128)}, f32[7,5,2,256]{3,1,2,0:T(8,128)}, u32[]{:S(2)}, u32[]{:S(2)}) collective-permute-start(f32[7,5,2,256]{3,1,2,0:T(8,128)} %get-tuple-element.24), channel_id=1, source_target_pairs={{1,0},{2,1},{3,2},{4,3},{5,4},{6,5},{7,6},{8,7},{9,8},{10,9},{11,1... | collective-permute-start | bytes 215048 | tf_op jit(solution)/shard_map/ppermute | solution.py:30
  22.9 31.5 %collective-permute-start.2 = (f32[7,5,2,256]{3,1,2,0:T(8,128)}, f32[7,5,2,256]{3,1,2,0:T(8,128)}, u32[]{:S(2)}, u32[]{:S(2)}) collective-permute-start(f32[7,5,2,256]{3,1,2,0:T(8,128)} %get-tuple-element.25), channel_id=1, source_target_pairs={{0,1},{1,2},{2,3},{3,4},{4,5},{5,6},{6,7},{7,8},{8,9},{9,10},{10,1... | collective-permute-start | bytes 215048 | tf_op jit(solution)/shard_map/ppermute | solution.py:29
  27.4 19.1 %collective-permute-start = (f32[7,5,32]{1,0,2:T(8,128)}, f32[7,5,32]{1,0,2:T(8,128)}, u32[]{:S(2)}, u32[]{:S(2)}) collective-permute-start(f32[7,5,32]{1,0,2:T(8,128)} %bitcast.8), channel_id=1, source_target_pairs={{0,256},{256,512},{512,768},{1,257},{257,513},{513,769},{2,258},{2... | collective-permute-start | bytes 13448 | tf_op jit(solution)/shard_map/ppermute | solution.py:19
  31.1 1.4 %copy-start.12 = (f32[4]{0:T(128)S(1)}, f32[4]{0:T(128)}, u32[]{:S(2)}) copy-start(f32[4]{0:T(128)} %param.11) | copy-start | bytes 52
  31.1 2.7 %copy-start.8 = (s32[4,3]{1,0:T(4,128)S(1)}, s32[4,3]{1,0:T(4,128)}, u32[]{:S(2)}) copy-start(s32[4,3]{1,0:T(4,128)} %param.10) | copy-start | bytes 148
  31.1 5.1 %copy-start.7 = (f32[7]{0:T(128)S(1)}, f32[7]{0:T(128)}, u32[]{:S(2)}) copy-start(f32[7]{0:T(128)} %constant.18.clone.1) | copy-start | bytes 88
  31.1 5.3 %copy-start = (f32[1,7,5,32,256]{4,3,2,1,0:T(8,128)S(1)}, f32[1,7,5,32,256]{4,3,2,1,0:T(8,128)}, u32[]{:S(2)}) copy-start(f32[1,7,5,32,256]{4,3,2,1,0:T(8,128)} %param.7) | copy-start | bytes 3440644
  33.8 5.7 %copy-start.6 = (f32[7,5,32]{2,0,1:T(8,128)S(1)}, f32[7,5,32]{2,0,1:T(8,128)}, u32[]{:S(2)}) copy-start(f32[7,5,32]{2,0,1:T(8,128)} %param.12) | copy-start | bytes 13444
  39.3 11.0 %copy-start.9 = (pred[32]{0:T(512)(128)(4,1)S(1)}, pred[32]{0:T(512)(128)(4,1)}, u32[]{:S(2)}) copy-start(pred[32]{0:T(512)(128)(4,1)} %compare_and_fusion) | copy-start | bytes 100
  40.3 6.3 %copy-start.5 = (f32[7,5,32]{1,0,2:T(8,128)S(1)}, f32[7,5,32]{1,0,2:T(8,128)}, u32[]{:S(2)}) copy-start(f32[7,5,32]{1,0,2:T(8,128)} %copy.39) | copy-start | bytes 13444
  60.4 1.2 %copy-start.1 = (f32[5,32,256]{2,0,1:T(8,128)S(1)}, f32[5,32,256]{2,0,1:T(8,128)}, u32[]{:S(2)}) copy-start(f32[5,32,256]{2,0,1:T(8,128)} %copy.47) | copy-start | bytes 491524
  60.4 1.2 %copy-start.2 = (f32[5,32,256]{2,0,1:T(8,128)S(1)}, f32[5,32,256]{2,0,1:T(8,128)}, u32[]{:S(2)}) copy-start(f32[5,32,256]{2,0,1:T(8,128)} %copy.46) | copy-start | bytes 491524
  60.4 1.2 %copy-start.3 = (f32[5,32,256]{2,0,1:T(8,128)S(1)}, f32[5,32,256]{2,0,1:T(8,128)}, u32[]{:S(2)}) copy-start(f32[5,32,256]{2,0,1:T(8,128)} %copy.45) | copy-start | bytes 491524
  63.5 21.7 %copy-start.4 = (f32[1,7,5,32,1]{4,2,3,1,0:T(8,128)S(1)}, f32[1,7,5,32,1]{4,2,3,1,0:T(8,128)}, u32[]{:S(2)}) copy-start(f32[1,7,5,32,1]{4,2,3,1,0:T(8,128)} %copy.41) | copy-start | bytes 13444
  63.5 21.7 %copy-start.10 = (f32[1,5,5]{2,0,1:T(1,128)S(1)}, f32[1,5,5]{2,0,1:T(1,128)}, u32[]{:S(2)}) copy-start(f32[1,5,5]{2,0,1:T(1,128)} %param.9) | copy-start | bytes 304
  63.5 14.0 %collective-permute-start.3 = (f32[7,5,2,256]{3,1,2,0:T(8,128)S(1)}, f32[7,5,2,256]{3,1,2,0:T(8,128)S(1)}, u32[]{:S(2)}, u32[]{:S(2)}) collective-permute-start(f32[7,5,2,256]{3,1,2,0:T(8,128)S(1)} %get-tuple-element.17), channel_id=1, source_target_pairs={{1,0},{2,1},{3,2},{4,3},{5,4},{6,5},{7,6},{8,7},{9,8},{10,9},{11,1... | collective-permute-start | bytes 215048 | tf_op jit(solution)/shard_map/ppermute | solution.py:30
  73.6 11.5 %collective-permute-start.4 = (f32[7,5,2,256]{3,1,2,0:T(8,128)S(1)}, f32[7,5,2,256]{3,1,2,0:T(8,128)S(1)}, u32[]{:S(2)}, u32[]{:S(2)}) collective-permute-start(f32[7,5,2,256]{3,1,2,0:T(8,128)S(1)} %get-tuple-element.18), channel_id=1, source_target_pairs={{0,1},{1,2},{2,3},{3,4},{4,5},{5,6},{6,7},{7,8},{8,9},{9,10},{10,1... | collective-permute-start | bytes 215048 | tf_op jit(solution)/shard_map/ppermute | solution.py:29
  93.0 8.8 %collective-permute-start.5 = (f32[7,5,2,256]{3,1,2,0:T(8,128)S(1)}, f32[7,5,2,256]{3,1,2,0:T(8,128)S(1)}, u32[]{:S(2)}, u32[]{:S(2)}) collective-permute-start(f32[7,5,2,256]{3,1,2,0:T(8,128)S(1)} %get-tuple-element.10), channel_id=1, source_target_pairs={{1,0},{2,1},{3,2},{4,3},{5,4},{6,5},{7,6},{8,7},{9,8},{10,9},{11,1... | collective-permute-start | bytes 215048 | tf_op jit(solution)/shard_map/ppermute | solution.py:30
  94.9 12.6 %collective-permute-start.6 = (f32[7,5,2,256]{3,1,2,0:T(8,128)S(1)}, f32[7,5,2,256]{3,1,2,0:T(8,128)S(1)}, u32[]{:S(2)}, u32[]{:S(2)}) collective-permute-start(f32[7,5,2,256]{3,1,2,0:T(8,128)S(1)} %get-tuple-element.11), channel_id=1, source_target_pairs={{0,1},{1,2},{2,3},{3,4},{4,5},{5,6},{6,7},{7,8},{8,9},{9,10},{10,1... | collective-permute-start | bytes 215048 | tf_op jit(solution)/shard_map/ppermute | solution.py:29
where the time goes:
time: 117 us; the launch traced here: 116 us
  starting transfers between devices  44.5 us (38%)
  local copies, waits for them, and re-layouts  26 us (22%)
  matrix products  22.6 us (19%)
  waiting for transfers between devices  13.3 us (11%)
  other arithmetic  9.58 us (8%)
    ppermute x3, starting transfers between devices, padded_2(): after = lax.ppermute(first, axis, down)  32.3 us
    dot_general x3, matrix products, section_residual(): jnp.einsum('ab,tbwl->tawl', flux_jac, centre - before, precision=largest_...  15.5 us
    ppermute x3, waiting for transfers between devices, padded_2(): before = lax.ppermute(last, axis, up)  13.3 us
    ppermute x3, starting transfers between devices, padded_2(): before = lax.ppermute(last, axis, up)  9.11 us
    dot_general x3, matrix products, section_residual(): jnp.einsum('ts,svwl->tvwl', spectral_derivative, centre, precision=larges...  6.51 us
    mul x4, local copies, waits for them, and re-layouts, apply_block(): inverse[None, :, column_index] * residual[:, column_index][:, None]  6.17 us
    sub x3, other arithmetic, body(): local_state - section_weight * apply_block(local_inverse, residual)  4.87 us
    slice x3, local copies, waits for them, and re-layouts, apply_block(): total = inverse[None, :, 0] * residual[:, 0][:, None]  3.13 us
  transfers between devices with their start and end apart: 7, of which 2 were waited for; matrix products, arithmetic and copies ran while one was open for 26% of the time, Pallas kernels for 0%

commit v1 on v0

v1 whole, which is shorter than its diff:
```python
import math

import jax
import jax.numpy as jnp
from jax import lax
from jax.experimental import pallas as pl
from jax.experimental.pallas import tpu as pltpu
from jax.sharding import PartitionSpec as P


TIMES = 7
VARS = 5
TV = TIMES * VARS
VV = VARS * VARS
SECTIONS = 3
LANES = 128
HALVES = 2
DEEP = 6
NEAR = 4
LINES = 32
S_ROWS = HALVES * TV * DEEP
I_ROWS = HALVES * VV * NEAR
MSG = S_ROWS + I_ROWS + NEAR

nu_second = 0.25
nu_fourth = 0.03
time_scale = 0.05

COS7 = [math.cos(2.0 * math.pi * k / 7.0) for k in range(7)]
SIN7 = [math.sin(2.0 * math.pi * k / 7.0) for k in range(7)]


def pick(table, index):
    value = jnp.float32(table[0])
    for k in range(1, 7):
        value = jnp.where(index == k, jnp.float32(table[k]), value)
    return value


def pack_message(out, s_ref, i_ref, s_from, i_from):
    for h in range(HALVES):
        cut = pl.ds(h * LANES, LANES)
        for k in range(TV):
            out[pl.ds((h * TV + k) * DEEP, DEEP), :] = s_ref[k, pl.ds(s_from, DEEP), cut]
        for k in range(VV):
            out[pl.ds(S_ROWS + (h * VV + k) * NEAR, NEAR), :] = i_ref[k, pl.ds(i_from, NEAR), cut]


def pack_kernel(pair_ref, state, inverse, inflow, up, outlet, s_hi, i_hi, last, flow, turned, sems):
    copies = [
        pltpu.make_async_copy(state.at[:, pl.ds(LINES - 8, 8), :], s_hi, sems.at[0]),
        pltpu.make_async_copy(inverse.at[:, pl.ds(LINES - 8, 8), :], i_hi, sems.at[1]),
        pltpu.make_async_copy(state.at[:, :, pl.ds(LANES, LANES)], last, sems.at[2]),
    ]
    for copy in copies:
        copy.start()
    copies[0].wait()
    copies[1].wait()
    pack_message(up, s_hi, i_hi, 8 - DEEP, 8 - NEAR)
    start_line = lax.axis_index("mesh") * LINES
    for j in range(NEAR):
        pair = (pair_ref[0, LINES - NEAR + j] - start_line).astype(jnp.float32)
        up[pl.ds(S_ROWS + I_ROWS + j, 1), :] = jnp.full((1, LANES), pair, jnp.float32)
    copies[2].wait()
    lane = lax.broadcasted_iota(jnp.int32, (LINES, LANES), 1)
    total = jnp.zeros((LINES, LANES), jnp.float32)
    for k in range(TV):
        total = jnp.where(lane == k, pltpu.roll(last[k], k + 1, 1), total)
    outlet[...] = total

    @pl.when(lax.axis_index("row") == lax.axis_size("row") - 1)
    def _():
        copy = pltpu.make_async_copy(inflow, flow, sems.at[3])
        copy.start()
        turned[...] = jnp.zeros((LANES, LANES), jnp.float32)
        copy.wait()
        for t in range(TIMES):
            for v in range(VARS):
                turned[pl.ds(t * VARS + v, 1), pl.ds(0, LINES)] = flow[v, pl.ds(t, 1), :]
        outlet[...] = jnp.transpose(turned[...])[:LINES, :]


F32 = jnp.float32
SMEM = pl.BlockSpec(memory_space=pltpu.SMEM)
VMEM = pl.BlockSpec(memory_space=pltpu.VMEM)
HBM = pl.BlockSpec(memory_space=pltpu.HBM)


def pack(pairing, state, inverse, inflow):
    return pl.pallas_call(
        pack_kernel,
        out_shape=(
            jax.ShapeDtypeStruct((MSG, LANES), F32),
            jax.ShapeDtypeStruct((LINES, LANES), F32),
        ),
        in_specs=[SMEM, HBM, HBM, HBM],
        out_specs=[VMEM] * 2,
        scratch_shapes=[
            pltpu.VMEM((TV, 8, HALVES * LANES), F32),
            pltpu.VMEM((VV, 8, HALVES * LANES), F32),
            pltpu.VMEM((TV, LINES, LANES), F32),
            pltpu.VMEM((VARS, TIMES, LINES), F32),
            pltpu.VMEM((LANES, LANES), F32),
            pltpu.SemaphoreType.DMA((4,)),
        ],
        name="pack",
        compiler_params=pltpu.CompilerParams(vmem_limit_bytes=4 << 20),
        cost_estimate=pl.CostEstimate(flops=10000, bytes_accessed=1_500_000, transcendentals=0),
    )(pairing, state, inverse, inflow)


def section_weights(flux, spectral, weight):
    w = jnp.float32(weight)
    scaled = [[flux[0, a, b] * w for b in range(VARS)] for a in range(VARS)]
    return scaled, [d * w for d in spectral]


def block_update(src, base, inv, ghost, r0, scaled, spectral, weight, emit):
    first = lax.broadcasted_iota(jnp.int32, (8, LANES), 1) == 0
    centre_c = jnp.float32((2.0 * nu_second + 6.0 * nu_fourth) * weight)
    near_c = jnp.float32((-nu_second - 4.0 * nu_fourth) * weight)
    far_c = jnp.float32(nu_fourth * weight)
    for h in range(HALVES):
        for t in range(TIMES):
            diffs = []
            for v in range(VARS):
                k = t * VARS + v
                here = src[h * TV + k, pl.ds(r0, 8), :]
                turned = pltpu.roll(here, 1, 1)
                if h == 0:
                    edge = ghost[k, pl.ds(r0, 8), :]
                else:
                    edge = pltpu.roll(src[k, pl.ds(r0, 8), :], 1, 1)
                diffs.append(here - jnp.where(first, edge, turned))
            residual = []
            for v in range(VARS):
                p = h * TV + t * VARS + v
                here = src[p, pl.ds(r0, 8), :]
                near = src[p, pl.ds(r0 - 1, 8), :] + src[p, pl.ds(r0 + 1, 8), :]
                far = src[p, pl.ds(r0 - 2, 8), :] + src[p, pl.ds(r0 + 2, 8), :]
                value = centre_c * here + near_c * near + far_c * far
                for j in range(1, 4):
                    early = src[h * TV + ((t - j) % TIMES) * VARS + v, pl.ds(r0, 8), :]
                    late = src[h * TV + ((t + j) % TIMES) * VARS + v, pl.ds(r0, 8), :]
                    value = value + spectral[j - 1] * (early - late)
                for b in range(VARS):
                    value = value + scaled[v][b] * diffs[b]
                residual.append(value)
            for v in range(VARS):
                p = h * TV + t * VARS + v
                value = base[p, pl.ds(r0, 8), :]
                for b in range(VARS):
                    value = value - inv[h * VV + v * VARS + b, pl.ds(r0, 8), :] * residual[b]
                emit(h, t * VARS + v, value)


def transfer_weights(modes_ref, delay_ref):
    row = lax.axis_index("row")
    upstream = jnp.maximum(row - 1, 0)
    delay = delay_ref[row]
    waves = []
    for j in range(3):
        mode = modes_ref[upstream, j]
        phase = jnp.full((8, LANES), mode.astype(jnp.float32) * delay, jnp.float32)
        phase = (phase - jnp.round(phase)) * jnp.float32(2.0 * math.pi)
        waves.append((lax.rem(mode, 7), jnp.cos(phase), jnp.sin(phase)))
    weights = []
    for d in range(TIMES):
        weight = jnp.full((8, LANES), 1.0 / 7.0, jnp.float32)
        for rest, cosine, sine in waves:
            index = lax.rem(rest * d, 7)
            weight = weight + jnp.float32(2.0 / 7.0) * (cosine * pick(COS7, index) - sine * pick(SIN7, index))
        weights.append(weight)
    return weights


def transfer(paired, weights):
    doubled = paired + pltpu.roll(paired, TV, 1)
    total = weights[0] * doubled
    for d in range(1, TIMES):
        total = total + weights[d] * pltpu.roll(doubled, VARS * d, 1)
    return total


def to_lane_zero(values, k):
    return pltpu.roll(values, LANES - TV - k, 1)


def spectral_scalars(modes_ref):
    row = lax.axis_index("row")
    rates = []
    for k in range(1, 4):
        total = jnp.float32(0.0)
        for j in range(3):
            mode = modes_ref[row, j]
            index = lax.rem(lax.rem(mode, 7) * k, 7)
            total = total + mode.astype(jnp.float32) * pick(SIN7, index)
        rates.append(total * jnp.float32(-time_scale * 2.0 * math.pi * 2.0 / 7.0))
    return rates


def goes_first():
    place = lax.axis_index("mesh")
    return lax.rem(place, 32) < 2


OUT_SHAPE = jax.ShapeDtypeStruct((TV, LINES, HALVES * LANES), F32)
FIELD = jax.ShapeDtypeStruct((HALVES * TV, LINES, LANES), F32)


def inner(pair_ref, flux, modes_ref, weights, state, inverse, mid, out, q0, inv, ghost, q1, q2, q3, paired, sems, out_sems):
    loads = []
    for h in range(HALVES):
        cut = pl.ds(h * LANES, LANES)
        loads.append(pltpu.make_async_copy(state.at[:, :, cut], q0.at[pl.ds(h * TV, TV)], sems.at[h]))
        loads.append(pltpu.make_async_copy(inverse.at[:, :, cut], inv.at[pl.ds(h * VV, VV)], sems.at[2 + h]))
    for copy in loads:
        copy.start()
    rates = spectral_scalars(modes_ref)
    start_line = lax.axis_index("mesh") * LINES
    for w in range(LINES):
        paired[pl.ds(w, 1), :] = mid[pl.ds(pair_ref[0, w] - start_line, 1), :]
    for w in range(0, LINES, 8):
        values = transfer(paired[pl.ds(w, 8), :], weights)
        for k in range(TV):
            ghost[k, pl.ds(w, 8), :] = to_lane_zero(values, k)
    for copy in loads:
        copy.wait()

    def section(src, dst, number, count, first, stop):
        weight = (number + 1.0) / SECTIONS
        scaled, spectral = section_weights(flux, rates, weight)

        def body(i, carry):
            r0 = jnp.minimum(first + i * 8, stop - 8)

            def emit(h, k, value):
                dst[h * TV + k, pl.ds(r0, 8), :] = value

            block_update(src, q0, inv, ghost, r0, scaled, spectral, weight, emit)
            return carry

        lax.fori_loop(0, count, body, 0)

    section(q0, q1, 0, 4, 2, LINES - 2)
    section(q1, q2, 1, 3, 4, LINES - 4)
    scaled, spectral = section_weights(flux, rates, 1.0)

    def results(i, h):
        at = pl.ds(pl.multiple_of(8 + i * 8, 8), 8)
        return pltpu.make_async_copy(
            q3.at[pl.ds(h * TV, TV), at, :], out.at[:, at, pl.ds(h * LANES, LANES)], out_sems.at[i, h]
        )

    def last(i, carry):
        r0 = pl.multiple_of(8 + i * 8, 8)

        def emit(h, k, value):
            q3[h * TV + k, pl.ds(r0, 8), :] = value

        block_update(q2, q0, inv, ghost, r0, scaled, spectral, 1.0, emit)
        for h in range(HALVES):
            results(i, h).start()
        return carry

    lax.fori_loop(0, 2, last, 0)
    for i in range(2):
        for h in range(HALVES):
            results(i, h).wait()


INNER_SHAPES = (
    OUT_SHAPE,
    FIELD,
    jax.ShapeDtypeStruct((HALVES * VV, LINES, LANES), F32),
    jax.ShapeDtypeStruct((TV, LINES, LANES), F32),
    FIELD,
    FIELD,
)
INNER_SCRATCH = [
    pltpu.VMEM((HALVES * TV, LINES, LANES), F32),
    pltpu.VMEM((LINES, LANES), F32),
    pltpu.SemaphoreType.DMA((4,)),
    pltpu.SemaphoreType.DMA((2, HALVES)),
]


def early_kernel(
    pair_ref, flux, modes_ref, delay_ref, state, inverse, mid,
    down, weights_ref, out, q0, inv, ghost, q1, q2, s_lo, i_lo, low_sems, q3, paired, sems, out_sems,
):
    lows = [
        pltpu.make_async_copy(state.at[:, pl.ds(0, 8), :], s_lo, low_sems.at[0]),
        pltpu.make_async_copy(inverse.at[:, pl.ds(0, 8), :], i_lo, low_sems.at[1]),
    ]
    for copy in lows:
        copy.start()
    start_line = lax.axis_index("mesh") * LINES
    weights = transfer_weights(modes_ref, delay_ref)
    for d in range(TIMES):
        weights_ref[d] = weights[d]
    for w in range(8):
        paired[pl.ds(w, 1), :] = mid[pl.ds(pair_ref[0, w] - start_line, 1), :]
    down[pl.ds(S_ROWS + I_ROWS, NEAR), :] = transfer(paired[pl.ds(0, 8), :], weights)[:NEAR, :]
    for copy in lows:
        copy.wait()
    pack_message(down, s_lo, i_lo, 0, 0)

    @pl.when(goes_first())
    def _():
        again = [weights_ref[d] for d in range(TIMES)]
        inner(
            pair_ref, flux, modes_ref, again, state, inverse, mid,
            out, q0, inv, ghost, q1, q2, q3, paired, sems, out_sems,
        )


def early(pairing, flux, modes, delay, state, inverse, mid):
    return pl.pallas_call(
        early_kernel,
        out_shape=(
            jax.ShapeDtypeStruct((MSG, LANES), F32),
            jax.ShapeDtypeStruct((TIMES, 8, LANES), F32),
        ) + INNER_SHAPES,
        in_specs=[SMEM] * 4 + [HBM] * 2 + [VMEM],
        out_specs=[VMEM, VMEM, HBM] + [VMEM] * 5,
        scratch_shapes=[
            pltpu.VMEM((TV, 8, HALVES * LANES), F32),
            pltpu.VMEM((VV, 8, HALVES * LANES), F32),
            pltpu.SemaphoreType.DMA((2,)),
        ] + INNER_SCRATCH,
        name="early",
        compiler_params=pltpu.CompilerParams(vmem_limit_bytes=10 << 20),
        cost_estimate=pl.CostEstimate(flops=30_000_000, bytes_accessed=3_000_000, transcendentals=0),
    )(pairing, flux, modes, delay, state, inverse, mid)


def late_kernel(
    pair_ref, flux, modes_ref, weights_ref, state, inverse, mid, _,
    out, q0, inv, ghost, q1, q2, q3, paired, sems, out_sems,
):
    @pl.when(jnp.logical_not(goes_first()))
    def _():
        weights = [weights_ref[d] for d in range(TIMES)]
        inner(
            pair_ref, flux, modes_ref, weights, state, inverse, mid,
            out, q0, inv, ghost, q1, q2, q3, paired, sems, out_sems,
        )


def late(pairing, flux, modes, weights, state, inverse, mid, out):
    return pl.pallas_call(
        late_kernel,
        out_shape=INNER_SHAPES,
        in_specs=[SMEM] * 3 + [VMEM] + [HBM] * 2 + [VMEM] + [HBM],
        out_specs=[HBM] + [VMEM] * 5,
        scratch_shapes=INNER_SCRATCH,
        input_output_aliases={7: 0},
        name="late",
        compiler_params=pltpu.CompilerParams(vmem_limit_bytes=10 << 20),
        cost_estimate=pl.CostEstimate(flops=30_000_000, bytes_accessed=3_000_000, transcendentals=0),
    )(pairing, flux, modes, weights, state, inverse, mid, out)


STRIP = 16


class Side:
    def __init__(self, low):
        if low:
            self.shift, self.halo, self.near = 22, 10, 10
            self.block, self.final, self.own = 6, 2, LINES - 8
            self.mine = (24, 8), (26, 2), (22, 6)
        else:
            self.shift, self.halo, self.near = -6, 0, 2
            self.block, self.final, self.own = 2, 6, 0
            self.mine = (0, 8), (4, 2), (4, 6)

    def rows(self, which):
        line, many = self.mine[which]
        return pl.ds(line - self.shift, many), pl.ds(line, many)


def edges_kernel(
    flux, modes_ref, weights_ref, got_dn, got_up, source, *rest,
):
    set_a, set_b, (_, out, *strips, sems) = rest[:5], rest[5:10], rest[10:]
    sides = []
    for at, (low, got) in enumerate(((True, got_dn), (False, got_up))):
        sides.append((Side(low), got, strips[6 * at : 6 * at + 6]))

    def bring(q0, inv, ghost, q1, q2):
        for side, _, (x0, x1, x2, iv, gh, x3) in sides:
            for which, dst, src in ((0, x0, q0), (0, iv, inv), (0, gh, ghost), (1, x1, q1), (2, x2, q2)):
                to, at = side.rows(which)
                for p in range(src.shape[0]):
                    dst[p, to, :] = src[p, at, :]

    first = goes_first()
    pl.when(first)(lambda: bring(*set_a))
    pl.when(jnp.logical_not(first))(lambda: bring(*set_b))
    lines = lax.broadcasted_iota(jnp.int32, (LINES, LANES), 0).astype(jnp.float32)
    chosen = []
    for j in range(NEAR):
        hit = lines == got_up[pl.ds(S_ROWS + I_ROWS + j, 1), :]
        chosen.append(jnp.sum(jnp.where(hit, source[...], 0.0), axis=0, keepdims=True))
    chosen = jnp.concatenate(chosen + [jnp.zeros((8 - NEAR, LANES), jnp.float32)], axis=0)
    chosen = transfer(chosen, [weights_ref[d] for d in range(TIMES)])[:NEAR, :]
    given = got_dn[pl.ds(S_ROWS + I_ROWS, NEAR), :]
    rates = spectral_scalars(modes_ref)
    for (side, got, (x0, x1, x2, iv, gh, x3)), values in zip(sides, (given, chosen)):
        for k in range(TV):
            gh[k, pl.ds(side.near, NEAR), :] = to_lane_zero(values, k)
        for p in range(HALVES * TV):
            x0[p, pl.ds(side.halo, DEEP), :] = got[pl.ds(p * DEEP, DEEP), :]
        for p in range(HALVES * VV):
            iv[p, pl.ds(side.near, NEAR), :] = got[pl.ds(S_ROWS + p * NEAR, NEAR), :]
    copies = []
    for at, (side, got, (x0, x1, x2, iv, gh, x3)) in enumerate(sides):
        for s, (src, dst) in enumerate(((x0, x1), (x1, x2))):
            weight = (s + 1.0) / SECTIONS
            scaled, spectral = section_weights(flux, rates, weight)

            def emit(h, k, value):
                dst[h * TV + k, pl.ds(side.block, 8), :] = value

            block_update(src, x0, iv, gh, side.block, scaled, spectral, weight, emit)
        scaled, spectral = section_weights(flux, rates, 1.0)

        def emit_last(h, k, value):
            x3[h * TV + k] = value

        block_update(x2, x0, iv, gh, side.final, scaled, spectral, 1.0, emit_last)
        for h in range(HALVES):
            copies.append(
                pltpu.make_async_copy(
                    x3.at[pl.ds(h * TV, TV)],
                    out.at[:, pl.ds(side.own, 8), pl.ds(h * LANES, LANES)],
                    sems.at[at, h],
                )
            )
            copies[-1].start()
    for copy in copies:
        copy.wait()


def edges(flux, modes, weights, got_dn, got_up, source, sets, out):
    return pl.pallas_call(
        edges_kernel,
        out_shape=OUT_SHAPE,
        in_specs=[SMEM] * 2 + [VMEM] * 14 + [HBM],
        out_specs=HBM,
        scratch_shapes=[
            pltpu.VMEM((HALVES * TV, STRIP, LANES), F32),
            pltpu.VMEM((HALVES * TV, STRIP, LANES), F32),
            pltpu.VMEM((HALVES * TV, STRIP, LANES), F32),
            pltpu.VMEM((HALVES * VV, STRIP, LANES), F32),
            pltpu.VMEM((TV, STRIP, LANES), F32),
            pltpu.VMEM((HALVES * TV, 8, LANES), F32),
        ] * 2 + [pltpu.SemaphoreType.DMA((2, HALVES))],
        input_output_aliases={16: 0},
        name="edges",
        compiler_params=pltpu.CompilerParams(vmem_limit_bytes=10 << 20),
        cost_estimate=pl.CostEstimate(flops=20_000_000, bytes_accessed=1_000_000, transcendentals=0),
    )(flux, modes, weights, got_dn, got_up, source, *sets, out)


def steps(state, inverse_blocks, flux_jacobian, harmonics, interface_delay, inflow, pairing):
    rows, devices = lax.axis_size("row"), lax.axis_size("mesh")
    local_state = state.reshape(TV, LINES, HALVES * LANES)
    local_inverse = inverse_blocks.reshape(VV, LINES, HALVES * LANES)
    local_state, local_inverse, flow, pairing = (
        pltpu.with_memory_space_constraint(array, pltpu.HBM)
        for array in (local_state, local_inverse, inflow.transpose(1, 0, 2), pairing)
    )
    up, outlet = pack(pairing, local_state, local_inverse, flow)
    onward = [(i, i + 1) for i in range(devices - 1)]
    back = [(j, i) for i, j in onward]

    def downstream(step):
        return [
            (r * devices + m, ((r + 1) % rows) * devices + m + step)
            for r in range(rows)
            for m in range(devices)
            if 0 <= m + step < devices
        ]

    mid = lax.ppermute(outlet, ("row", "mesh"), downstream(0))
    got_up = lax.ppermute(up, "mesh", onward)
    down, weights, out, *set_a = early(
        pairing, flux_jacobian, harmonics, interface_delay, local_state, local_inverse, mid
    )
    got_dn = lax.ppermute(down, "mesh", back)
    above = lax.ppermute(outlet, ("row", "mesh"), downstream(1))
    out, *set_b = late(pairing, flux_jacobian, harmonics, weights, local_state, local_inverse, mid, out)
    out = edges(flux_jacobian, harmonics, weights, got_dn, got_up, above, [*set_a, *set_b], out)
    return out.reshape(state.shape)


def solution(mesh):
    return jax.shard_map(
        steps,
        mesh=mesh,
        in_specs=(
            P("row", None, None, "mesh", None),
            P("row", None, None, "mesh", None),
            P("row", None, None),
            P(),
            P(),
            P(None, None, "mesh"),
            P("row", "mesh"),
        ),
        out_specs=P("row", None, None, "mesh", None),
        check_vma=False,
    )
```

time: 117 us -> 45.3 us (0.39)
  local copies, waits for them, and re-layouts: 26 us -> 0.01 us
  starting transfers between devices: 44.5 us -> 20.1 us
  matrix products: 22.6 us -> 0 us
  Pallas kernels: 0 us -> 16.7 us
  other arithmetic: 9.58 us -> 0 us
  waiting for transfers between devices: 13.3 us -> 8.09 us
    ppermute x7 -> x4, starting transfers between devices: 44.5 us -> 20.1 us  [the longest x1 10.1 us: steps(): got_dn = lax.ppermute(down, 'mesh', back)]
    dot_general x9 -> x0, matrix products: 22.6 us -> none  [the longest x3 15.5 us: section_residual(): jnp.einsum('ab,tbwl->tawl', flux_jac, centre - before, precision=largest_...]
    pallas_call x0 -> x4, Pallas kernels: none -> 16.7 us  [the longest x1 9.39 us: early(): pl.pallas_call(early_kernel, out_shape=(jax.ShapeDtypeStruct((MSG, LANES)...]
    mul x6 -> x0, local copies, waits for them, and re-layouts: 8.37 us -> none  [the longest x4 6.17 us: apply_block(): inverse[None, :, column_index] * residual[:, column_index][:, None]]
    ppermute x7 -> x4, waiting for transfers between devices: 13.3 us -> 8.09 us  [the longest x1 8.08 us: steps(): above = lax.ppermute(outlet, ('row', 'mesh'), downstream(1))]
    sub x3 -> x0, other arithmetic: 4.87 us -> none  [body(): local_state - section_weight * apply_block(local_inverse, residual)]
    slice x7 -> x0, local copies, waits for them, and re-layouts: 4.19 us -> none  [the longest x3 3.13 us: apply_block(): total = inverse[None, :, 0] * residual[:, 0][:, None]]
    select_n x3 -> x0, other arithmetic: 3.24 us -> none  [the longest x2 1.67 us: body(): paired = jnp.take(upstream, local_pairs, axis=2)]
  transfers between devices with their start and end apart: 7 -> 4, of which waited for: 2 -> 1; matrix products, arithmetic and copies ran while one was open for 26% -> 0% of each run, Pallas kernels for 0% -> 23%
where the time goes in v1:
time: 45.3 us; the launch traced here: 45 us
  starting transfers between devices  20.1 us (44%)
  Pallas kernels  16.7 us (37%)
  waiting for transfers between devices  8.09 us (18%)
    ppermute x1, starting transfers between devices, steps(): got_dn = lax.ppermute(down, 'mesh', back)  10.1 us
    pallas_call x1, Pallas kernels, early(): pl.pallas_call(early_kernel, out_shape=(jax.ShapeDtypeStruct((MSG, LANES)...  9.39 us
    ppermute x1, waiting for transfers between devices, steps(): above = lax.ppermute(outlet, ('row', 'mesh'), downstream(1))  8.08 us
    ppermute x1, starting transfers between devices, steps(): got_up = lax.ppermute(up, 'mesh', onward)  4.36 us
    pallas_call x1, Pallas kernels, edges(): pl.pallas_call(edges_kernel, out_shape=OUT_SHAPE, in_specs=[SMEM] * 2 + [...  4.25 us
    ppermute x1, starting transfers between devices, steps(): mid = lax.ppermute(outlet, ('row', 'mesh'), downstream(0))  3.68 us
    pallas_call x1, Pallas kernels, pack(): pl.pallas_call(pack_kernel, out_shape=(jax.ShapeDtypeStruct((MSG, LANES),...  2.3 us
    ppermute x1, starting transfers between devices, steps(): above = lax.ppermute(outlet, ('row', 'mesh'), downstream(1))  1.92 us
  transfers between devices with their start and end apart: 4, of which 1 were waited for; matrix products, arithmetic and copies ran while one was open for 0% of the time, Pallas kernels for 23%

profile of v1, /device:TPU:33, one launch (start us, length us, event | category | flops | bytes accessed | tf_op | source)
XLA Modules:
  0.0 45.0 jit_solution(11802636796904279637)
XLA Ops:
  0.0 0.0 copy-start.2
  0.0 0.0 copy-start
  0.0 0.0 copy-start.1
  0.0 2.3 %pack.1 = (f32[624,128]{1,0:T(8,128)S(1)}, f32[32,128]{1,0:T(8,128)S(1)}) custom-call(s32[1,32]{1,0:T(1,128)} %pair_ref.5, f32[35,32,256]{2,1,0:T(8,128)} %bitcast.4, f32[25,32,256]{2,1,0:T(8,128)} %bitcast.7, f32[5,7,32]{2,1,0:T(8,128)} %bitcast.10), custom_call_target="tpu_custom_call" | custom-call | flops 10000 | bytes 1500000 | tf_op jit(solution)/shard_map/pack/pallas_call | solution.py:90
  2.3 3.7 %collective-permute-start = (f32[32,128]{1,0:T(8,128)S(1)}, f32[32,128]{1,0:T(8,128)S(1)}, u32[]{:S(2)}, u32[]{:S(2)}) collective-permute-start(f32[32,128]{1,0:T(8,128)S(1)} %get-tuple-element.21), channel_id=1, source_target_pairs={{0,256},{1,257},{2,258},{3,259},{4,260},{5,261},{6,262},{7,263},{8... | collective-permute-start | bytes 49160 | tf_op jit(solution)/shard_map/ppermute | solution.py:488
  6.0 4.4 %collective-permute-start.2 = (f32[624,128]{1,0:T(8,128)S(1)}, f32[624,128]{1,0:T(8,128)S(1)}, u32[]{:S(2)}, u32[]{:S(2)}) collective-permute-start(f32[624,128]{1,0:T(8,128)S(1)} %get-tuple-element.24), channel_id=1, source_target_pairs={{0,1},{1,2},{2,3},{3,4},{4,5},{5,6},{6,7},{7,8},{8,9},{9,10},{10,1... | collective-permute-start | bytes 958472 | tf_op jit(solution)/shard_map/ppermute | solution.py:489
  10.4 0.0 copy-done.2
  10.4 0.0 collective-permute-done.mid
  10.4 0.0 copy-done
  10.4 0.0 copy-done.1
  10.4 9.4 %early.1 = (f32[624,128]{1,0:T(8,128)S(1)}, f32[7,8,128]{2,1,0:T(8,128)S(1)}, f32[35,32,256]{2,1,0:T(8,128)}, f32[70,32,128]{2,1,0:T(8,128)S(1)}, f32[50,32,128]...) custom-call(s32[1,32]{1,0:T(1,128)} %pair_ref.5, ...), custom_call_target="tpu_custom_call" | custom-call | flops 30000000 | bytes 3000000 | tf_op jit(solution)/shard_map/early/pallas_call | solution.py:319
  19.8 10.1 %collective-permute-start.1 = (f32[624,128]{1,0:T(8,128)S(1)}, f32[624,128]{1,0:T(8,128)S(1)}, u32[]{:S(2)}, u32[]{:S(2)}) collective-permute-start(f32[624,128]{1,0:T(8,128)S(1)} %get-tuple-element.23), channel_id=1, source_target_pairs={{1,0},{2,1},{3,2},{4,3},{5,4},{6,5},{7,6},{8,7},{9,8},{10,9},{11,1... | collective-permute-start | bytes 958472 | tf_op jit(solution)/shard_map/ppermute | solution.py:493
  29.9 1.9 %collective-permute-start.3 = (f32[32,128]{1,0:T(8,128)S(1)}, f32[32,128]{1,0:T(8,128)S(1)}, u32[]{:S(2)}, u32[]{:S(2)}) collective-permute-start(f32[32,128]{1,0:T(8,128)S(1)} %get-tuple-element.21), channel_id=1, source_target_pairs={{0,257},{1,258},{2,259},{3,260},{4,261},{5,262},{6,263},{7,264},{8... | collective-permute-start | bytes 49160 | tf_op jit(solution)/shard_map/ppermute | solution.py:494
  31.9 0.8 %late.1 = (f32[35,32,256]{2,1,0:T(8,128)}, f32[70,32,128]{2,1,0:T(8,128)S(1)}, f32[50,32,128]{2,1,0:T(8,128)S(1)}, f32[35,32,128]{2,1,0:T(8,128)S(1)}, f32[70,32...) custom-call(s32[1,32]{1,0:T(1,128)} %pair_ref.5, f32[1,5,5]{2,1,0:T(8,128)S(1)} %copy.12.flux, ...), custom_call_target="tpu_custom_call", output_to_operand_aliasing={{0}: (7, {})} | custom-call | flops 30000000 | bytes 3000000 | tf_op jit(solution)/shard_map/late/pallas_call | solution.py:352
  32.6 8.1 %collective-permute-done.3.source = f32[32,128]{1,0:T(8,128)S(1)} collective-permute-done((f32[32,128]{1,0:T(8,128)S(1)}, f32[32,128]{1,0:T(8,128)S(1)}, u32[]{:S(2)}, u32[]{:S(2)}) %collective-permute-start.3) | collective-permute-done | bytes 16416 | tf_op jit(solution)/shard_map/ppermute | solution.py:494
  40.7 0.0 collective-permute-done.2.got_up
  40.7 0.0 collective-permute-done.1.got_dn
  40.7 4.2 %edges.1 = f32[35,32,256]{2,1,0:T(8,128)} custom-call(f32[1,5,5]{2,1,0:T(8,128)S(1)} %copy.12.flux, s32[4,3]{1,0:T(4,128)S(1)} %copy-done, f32[7,8,128]{2,1,0:T(8,128)S(1)} %get-tuple-element.22.weights_ref, f32[624,128]{1,0:T(8,128)S(1)} %collective-permute-done.1.got_dn, ...), custom_call_target="tpu_custom_call", output_to_operand_aliasing={{}: (16, {})} | custom-call | flops 20000000 | bytes 1000000 | tf_op jit(solution)/shard_map/edges/pallas_call | solution.py:448
  (1 shorter events, 0.0 us)
Async XLA Ops:
  0.0 10.4 %copy-start.2 = (f32[1,5,5]{2,0,1:T(1,128)S(1)}, f32[1,5,5]{2,0,1:T(1,128)}, u32[]{:S(2)}) copy-start(f32[1,5,5]{2,0,1:T(1,128)} %param.9) | copy-start | bytes 304
  0.0 10.4 %copy-start = (s32[4,3]{1,0:T(4,128)S(1)}, s32[4,3]{1,0:T(4,128)}, u32[]{:S(2)}) copy-start(s32[4,3]{1,0:T(4,128)} %modes_ref.5) | copy-start | bytes 148
  0.0 10.4 %copy-start.1 = (f32[4]{0:T(128)S(1)}, f32[4]{0:T(128)}, u32[]{:S(2)}) copy-start(f32[4]{0:T(128)} %delay_ref.1) | copy-start | bytes 52
  2.3 8.1 %collective-permute-start = (f32[32,128]{1,0:T(8,128)S(1)}, f32[32,128]{1,0:T(8,128)S(1)}, u32[]{:S(2)}, u32[]{:S(2)}) collective-permute-start(f32[32,128]{1,0:T(8,128)S(1)} %get-tuple-element.21), channel_id=1, source_target_pairs={{0,256},{1,257},{2,258},{3,259},{4,260},{5,261},{6,262},{7,263},{8... | collective-permute-start | bytes 49160 | tf_op jit(solution)/shard_map/ppermute | solution.py:488
  6.0 34.7 %collective-permute-start.2 = (f32[624,128]{1,0:T(8,128)S(1)}, f32[624,128]{1,0:T(8,128)S(1)}, u32[]{:S(2)}, u32[]{:S(2)}) collective-permute-start(f32[624,128]{1,0:T(8,128)S(1)} %get-tuple-element.24), channel_id=1, source_target_pairs={{0,1},{1,2},{2,3},{3,4},{4,5},{5,6},{6,7},{7,8},{8,9},{9,10},{10,1... | collective-permute-start | bytes 958472 | tf_op jit(solution)/shard_map/ppermute | solution.py:489
  19.8 20.9 %collective-permute-start.1 = (f32[624,128]{1,0:T(8,128)S(1)}, f32[624,128]{1,0:T(8,128)S(1)}, u32[]{:S(2)}, u32[]{:S(2)}) collective-permute-start(f32[624,128]{1,0:T(8,128)S(1)} %get-tuple-element.23), channel_id=1, source_target_pairs={{1,0},{2,1},{3,2},{4,3},{5,4},{6,5},{7,6},{8,7},{9,8},{10,9},{11,1... | collective-permute-start | bytes 958472 | tf_op jit(solution)/shard_map/ppermute | solution.py:493
  29.9 10.8 %collective-permute-start.3 = (f32[32,128]{1,0:T(8,128)S(1)}, f32[32,128]{1,0:T(8,128)S(1)}, u32[]{:S(2)}, u32[]{:S(2)}) collective-permute-start(f32[32,128]{1,0:T(8,128)S(1)} %get-tuple-element.21), channel_id=1, source_target_pairs={{0,257},{1,258},{2,259},{3,260},{4,261},{5,262},{6,263},{7,264},{8... | collective-permute-start | bytes 49160 | tf_op jit(solution)/shard_map/ppermute | solution.py:494

commit v2 on v1

--- a/solution.py
+++ b/solution.py
@@ -1,3 +1,4 @@
+import functools
 import math
 
 import jax
@@ -46,22 +47,10 @@
             out[pl.ds(S_ROWS + (h * VV + k) * NEAR, NEAR), :] = i_ref[k, pl.ds(i_from, NEAR), cut]
 
 
-def pack_kernel(pair_ref, state, inverse, inflow, up, outlet, s_hi, i_hi, last, flow, turned, sems):
-    copies = [
-        pltpu.make_async_copy(state.at[:, pl.ds(LINES - 8, 8), :], s_hi, sems.at[0]),
-        pltpu.make_async_copy(inverse.at[:, pl.ds(LINES - 8, 8), :], i_hi, sems.at[1]),
-        pltpu.make_async_copy(state.at[:, :, pl.ds(LANES, LANES)], last, sems.at[2]),
-    ]
-    for copy in copies:
-        copy.start()
-    copies[0].wait()
-    copies[1].wait()
-    pack_message(up, s_hi, i_hi, 8 - DEEP, 8 - NEAR)
-    start_line = lax.axis_index("mesh") * LINES
-    for j in range(NEAR):
-        pair = (pair_ref[0, LINES - NEAR + j] - start_line).astype(jnp.float32)
-        up[pl.ds(S_ROWS + I_ROWS + j, 1), :] = jnp.full((1, LANES), pair, jnp.float32)
-    copies[2].wait()
+def outlet_kernel(state, inflow, outlet, last, flow, turned, sems):
+    copy = pltpu.make_async_copy(state.at[:, :, pl.ds(LANES, LANES)], last, sems.at[0])
+    copy.start()
+    copy.wait()
     lane = lax.broadcasted_iota(jnp.int32, (LINES, LANES), 1)
     total = jnp.zeros((LINES, LANES), jnp.float32)
     for k in range(TV):
@@ -70,7 +59,7 @@
 
     @pl.when(lax.axis_index("row") == lax.axis_size("row") - 1)
     def _():
-        copy = pltpu.make_async_copy(inflow, flow, sems.at[3])
+        copy = pltpu.make_async_copy(inflow, flow, sems.at[1])
         copy.start()
         turned[...] = jnp.zeros((LANES, LANES), jnp.float32)
         copy.wait()
@@ -86,27 +75,22 @@
 HBM = pl.BlockSpec(memory_space=pltpu.HBM)
 
 
-def pack(pairing, state, inverse, inflow):
+def last_cells(state, inflow):
     return pl.pallas_call(
-        pack_kernel,
-        out_shape=(
-            jax.ShapeDtypeStruct((MSG, LANES), F32),
-            jax.ShapeDtypeStruct((LINES, LANES), F32),
-        ),
-        in_specs=[SMEM, HBM, HBM, HBM],
-        out_specs=[VMEM] * 2,
+        outlet_kernel,
+        out_shape=jax.ShapeDtypeStruct((LINES, LANES), F32),
+        in_specs=[HBM, HBM],
+        out_specs=VMEM,
         scratch_shapes=[
-            pltpu.VMEM((TV, 8, HALVES * LANES), F32),
-            pltpu.VMEM((VV, 8, HALVES * LANES), F32),
             pltpu.VMEM((TV, LINES, LANES), F32),
             pltpu.VMEM((VARS, TIMES, LINES), F32),
             pltpu.VMEM((LANES, LANES), F32),
-            pltpu.SemaphoreType.DMA((4,)),
+            pltpu.SemaphoreType.DMA((2,)),
         ],
-        name="pack",
+        name="outlet",
         compiler_params=pltpu.CompilerParams(vmem_limit_bytes=4 << 20),
-        cost_estimate=pl.CostEstimate(flops=10000, bytes_accessed=1_500_000, transcendentals=0),
-    )(pairing, state, inverse, inflow)
+        cost_estimate=pl.CostEstimate(flops=10000, bytes_accessed=600_000, transcendentals=0),
+    )(state, inflow)
 
 
 def section_weights(flux, spectral, weight):
@@ -287,23 +271,30 @@
 
 def early_kernel(
     pair_ref, flux, modes_ref, delay_ref, state, inverse, mid,
-    down, weights_ref, out, q0, inv, ghost, q1, q2, s_lo, i_lo, low_sems, q3, paired, sems, out_sems,
+    up, down, weights_ref, out, q0, inv, ghost, q1, q2,
+    s_hi, i_hi, s_lo, i_lo, tile_sems, q3, paired, sems, out_sems,
 ):
-    lows = [
-        pltpu.make_async_copy(state.at[:, pl.ds(0, 8), :], s_lo, low_sems.at[0]),
-        pltpu.make_async_copy(inverse.at[:, pl.ds(0, 8), :], i_lo, low_sems.at[1]),
+    top = pl.ds(LINES - 8, 8)
+    tiles = [
+        pltpu.make_async_copy(state.at[:, top, :], s_hi, tile_sems.at[0]),
+        pltpu.make_async_copy(inverse.at[:, top, :], i_hi, tile_sems.at[1]),
+        pltpu.make_async_copy(state.at[:, pl.ds(0, 8), :], s_lo, tile_sems.at[2]),
+        pltpu.make_async_copy(inverse.at[:, pl.ds(0, 8), :], i_lo, tile_sems.at[3]),
     ]
-    for copy in lows:
+    for copy in tiles:
         copy.start()
     start_line = lax.axis_index("mesh") * LINES
     weights = transfer_weights(modes_ref, delay_ref)
     for d in range(TIMES):
         weights_ref[d] = weights[d]
-    for w in range(8):
-        paired[pl.ds(w, 1), :] = mid[pl.ds(pair_ref[0, w] - start_line, 1), :]
+    for j in range(NEAR):
+        paired[pl.ds(j, 1), :] = mid[pl.ds(pair_ref[0, j] - start_line, 1), :]
+        paired[pl.ds(8 + j, 1), :] = mid[pl.ds(pair_ref[0, LINES - NEAR + j] - start_line, 1), :]
     down[pl.ds(S_ROWS + I_ROWS, NEAR), :] = transfer(paired[pl.ds(0, 8), :], weights)[:NEAR, :]
-    for copy in lows:
+    up[pl.ds(S_ROWS + I_ROWS, NEAR), :] = transfer(paired[pl.ds(8, 8), :], weights)[:NEAR, :]
+    for copy in tiles:
         copy.wait()
+    pack_message(up, s_hi, i_hi, 8 - DEEP, 8 - NEAR)
     pack_message(down, s_lo, i_lo, 0, 0)
 
     @pl.when(goes_first())
@@ -320,14 +311,17 @@
         early_kernel,
         out_shape=(
             jax.ShapeDtypeStruct((MSG, LANES), F32),
+            jax.ShapeDtypeStruct((MSG, LANES), F32),
             jax.ShapeDtypeStruct((TIMES, 8, LANES), F32),
         ) + INNER_SHAPES,
         in_specs=[SMEM] * 4 + [HBM] * 2 + [VMEM],
-        out_specs=[VMEM, VMEM, HBM] + [VMEM] * 5,
+        out_specs=[VMEM, VMEM, VMEM, HBM] + [VMEM] * 5,
         scratch_shapes=[
             pltpu.VMEM((TV, 8, HALVES * LANES), F32),
             pltpu.VMEM((VV, 8, HALVES * LANES), F32),
-            pltpu.SemaphoreType.DMA((2,)),
+            pltpu.VMEM((TV, 8, HALVES * LANES), F32),
+            pltpu.VMEM((VV, 8, HALVES * LANES), F32),
+            pltpu.SemaphoreType.DMA((4,)),
         ] + INNER_SCRATCH,
         name="early",
         compiler_params=pltpu.CompilerParams(vmem_limit_bytes=10 << 20),
@@ -381,74 +375,58 @@
         return pl.ds(line - self.shift, many), pl.ds(line, many)
 
 
-def edges_kernel(
-    flux, modes_ref, weights_ref, got_dn, got_up, source, *rest,
-):
-    set_a, set_b, (_, out, *strips, sems) = rest[:5], rest[5:10], rest[10:]
-    sides = []
-    for at, (low, got) in enumerate(((True, got_dn), (False, got_up))):
-        sides.append((Side(low), got, strips[6 * at : 6 * at + 6]))
+def edge_kernel(low, flux, modes_ref, got, *rest):
+    set_a, set_b, (_, out, x0, x1, x2, iv, gh, x3, sems) = rest[:5], rest[5:10], rest[10:]
+    side = Side(low)
 
     def bring(q0, inv, ghost, q1, q2):
-        for side, _, (x0, x1, x2, iv, gh, x3) in sides:
-            for which, dst, src in ((0, x0, q0), (0, iv, inv), (0, gh, ghost), (1, x1, q1), (2, x2, q2)):
-                to, at = side.rows(which)
-                for p in range(src.shape[0]):
-                    dst[p, to, :] = src[p, at, :]
+        for which, dst, src in ((0, x0, q0), (0, iv, inv), (0, gh, ghost), (1, x1, q1), (2, x2, q2)):
+            to, at = side.rows(which)
+            for p in range(src.shape[0]):
+                dst[p, to, :] = src[p, at, :]
 
     first = goes_first()
     pl.when(first)(lambda: bring(*set_a))
     pl.when(jnp.logical_not(first))(lambda: bring(*set_b))
-    lines = lax.broadcasted_iota(jnp.int32, (LINES, LANES), 0).astype(jnp.float32)
-    chosen = []
-    for j in range(NEAR):
-        hit = lines == got_up[pl.ds(S_ROWS + I_ROWS + j, 1), :]
-        chosen.append(jnp.sum(jnp.where(hit, source[...], 0.0), axis=0, keepdims=True))
-    chosen = jnp.concatenate(chosen + [jnp.zeros((8 - NEAR, LANES), jnp.float32)], axis=0)
-    chosen = transfer(chosen, [weights_ref[d] for d in range(TIMES)])[:NEAR, :]
-    given = got_dn[pl.ds(S_ROWS + I_ROWS, NEAR), :]
+    values = got[pl.ds(S_ROWS + I_ROWS, NEAR), :]
     rates = spectral_scalars(modes_ref)
-    for (side, got, (x0, x1, x2, iv, gh, x3)), values in zip(sides, (given, chosen)):
-        for k in range(TV):
-            gh[k, pl.ds(side.near, NEAR), :] = to_lane_zero(values, k)
-        for p in range(HALVES * TV):
-            x0[p, pl.ds(side.halo, DEEP), :] = got[pl.ds(p * DEEP, DEEP), :]
-        for p in range(HALVES * VV):
-            iv[p, pl.ds(side.near, NEAR), :] = got[pl.ds(S_ROWS + p * NEAR, NEAR), :]
-    copies = []
-    for at, (side, got, (x0, x1, x2, iv, gh, x3)) in enumerate(sides):
-        for s, (src, dst) in enumerate(((x0, x1), (x1, x2))):
-            weight = (s + 1.0) / SECTIONS
-            scaled, spectral = section_weights(flux, rates, weight)
-
-            def emit(h, k, value):
-                dst[h * TV + k, pl.ds(side.block, 8), :] = value
-
-            block_update(src, x0, iv, gh, side.block, scaled, spectral, weight, emit)
-        scaled, spectral = section_weights(flux, rates, 1.0)
-
-        def emit_last(h, k, value):
-            x3[h * TV + k] = value
-
-        block_update(x2, x0, iv, gh, side.final, scaled, spectral, 1.0, emit_last)
-        for h in range(HALVES):
-            copies.append(
-                pltpu.make_async_copy(
-                    x3.at[pl.ds(h * TV, TV)],
-                    out.at[:, pl.ds(side.own, 8), pl.ds(h * LANES, LANES)],
-                    sems.at[at, h],
-                )
-            )
-            copies[-1].start()
+    for k in range(TV):
+        gh[k, pl.ds(side.near, NEAR), :] = to_lane_zero(values, k)
+    for p in range(HALVES * TV):
+        x0[p, pl.ds(side.halo, DEEP), :] = got[pl.ds(p * DEEP, DEEP), :]
+    for p in range(HALVES * VV):
+        iv[p, pl.ds(side.near, NEAR), :] = got[pl.ds(S_ROWS + p * NEAR, NEAR), :]
+    for s, (src, dst) in enumerate(((x0, x1), (x1, x2))):
+        weight = (s + 1.0) / SECTIONS
+        scaled, spectral = section_weights(flux, rates, weight)
+
+        def emit(h, k, value):
+            dst[h * TV + k, pl.ds(side.block, 8), :] = value
+
+        block_update(src, x0, iv, gh, side.block, scaled, spectral, weight, emit)
+    scaled, spectral = section_weights(flux, rates, 1.0)
+
+    def emit_last(h, k, value):
+        x3[h * TV + k] = value
+
+    block_update(x2, x0, iv, gh, side.final, scaled, spectral, 1.0, emit_last)
+    copies = [
+        pltpu.make_async_copy(
+            x3.at[pl.ds(h * TV, TV)], out.at[:, pl.ds(side.own, 8), pl.ds(h * LANES, LANES)], sems.at[h]
+        )
+        for h in range(HALVES)
+    ]
+    for copy in copies:
+        copy.start()
     for copy in copies:
         copy.wait()
 
 
-def edges(flux, modes, weights, got_dn, got_up, source, sets, out):
+def edge(low, flux, modes, got, sets, out):
     return pl.pallas_call(
-        edges_kernel,
+        functools.partial(edge_kernel, low),
         out_shape=OUT_SHAPE,
-        in_specs=[SMEM] * 2 + [VMEM] * 14 + [HBM],
+        in_specs=[SMEM] * 2 + [VMEM] * 11 + [HBM],
         out_specs=HBM,
         scratch_shapes=[
             pltpu.VMEM((HALVES * TV, STRIP, LANES), F32),
@@ -457,12 +435,13 @@
             pltpu.VMEM((HALVES * VV, STRIP, LANES), F32),
             pltpu.VMEM((TV, STRIP, LANES), F32),
             pltpu.VMEM((HALVES * TV, 8, LANES), F32),
-        ] * 2 + [pltpu.SemaphoreType.DMA((2, HALVES))],
-        input_output_aliases={16: 0},
-        name="edges",
-        compiler_params=pltpu.CompilerParams(vmem_limit_bytes=10 << 20),
-        cost_estimate=pl.CostEstimate(flops=20_000_000, bytes_accessed=1_000_000, transcendentals=0),
-    )(flux, modes, weights, got_dn, got_up, source, *sets, out)
+            pltpu.SemaphoreType.DMA((HALVES,)),
+        ],
+        input_output_aliases={13: 0},
+        name="low" if low else "high",
+        compiler_params=pltpu.CompilerParams(vmem_limit_bytes=6 << 20),
+        cost_estimate=pl.CostEstimate(flops=10_000_000, bytes_accessed=1_000_000, transcendentals=0),
+    )(flux, modes, got, *sets, out)
 
 
 def steps(state, inverse_blocks, flux_jacobian, harmonics, interface_delay, inflow, pairing):
@@ -473,7 +452,7 @@
         pltpu.with_memory_space_constraint(array, pltpu.HBM)
         for array in (local_state, local_inverse, inflow.transpose(1, 0, 2), pairing)
     )
-    up, outlet = pack(pairing, local_state, local_inverse, flow)
+    outlet = last_cells(local_state, flow)
     onward = [(i, i + 1) for i in range(devices - 1)]
     back = [(j, i) for i, j in onward]
 
@@ -486,14 +465,15 @@
         ]
 
     mid = lax.ppermute(outlet, ("row", "mesh"), downstream(0))
-    got_up = lax.ppermute(up, "mesh", onward)
-    down, weights, out, *set_a = early(
+    up, down, weights, out, *set_a = early(
         pairing, flux_jacobian, harmonics, interface_delay, local_state, local_inverse, mid
     )
+    got_up = lax.ppermute(up, "mesh", onward)
     got_dn = lax.ppermute(down, "mesh", back)
-    above = lax.ppermute(outlet, ("row", "mesh"), downstream(1))
     out, *set_b = late(pairing, flux_jacobian, harmonics, weights, local_state, local_inverse, mid, out)
-    out = edges(flux_jacobian, harmonics, weights, got_dn, got_up, above, [*set_a, *set_b], out)
+    sets = [*set_a, *set_b]
+    out = edge(False, flux_jacobian, harmonics, got_up, sets, out)
+    out = edge(True, flux_jacobian, harmonics, got_dn, sets, out)
     return out.reshape(state.shape)
 
 

time: 45.3 us -> 43.6 us (0.962)
  the two profiles are of different devices: /device:TPU:33 before, /device:TPU:4 now
where the time goes in v2:
time: 43.6 us; the launch traced here: 43.3 us
  starting transfers between devices  18.3 us (42%)
  Pallas kernels  17.4 us (40%)
  waiting for transfers between devices  7.51 us (17%)
    ppermute x1, starting transfers between devices, steps(): got_dn = lax.ppermute(down, 'mesh', back)  14.4 us
    pallas_call x1, Pallas kernels, early(): pl.pallas_call(early_kernel, out_shape=(jax.ShapeDtypeStruct((MSG, LANES)...  9.68 us
    pallas_call x2, Pallas kernels, edge(): pl.pallas_call(functools.partial(edge_kernel, low), out_shape=OUT_SHAPE,...  5.65 us
    ppermute x1, waiting for transfers between devices, steps(): got_up = lax.ppermute(up, 'mesh', onward)  4.4 us
    ppermute x1, waiting for transfers between devices, steps(): mid = lax.ppermute(outlet, ('row', 'mesh'), downstream(0))  3.11 us
    ppermute x1, starting transfers between devices, steps(): mid = lax.ppermute(outlet, ('row', 'mesh'), downstream(0))  1.92 us
    ppermute x1, starting transfers between devices, steps(): got_up = lax.ppermute(up, 'mesh', onward)  1.92 us
    pallas_call x1, Pallas kernels, last_cells(): pl.pallas_call(outlet_kernel, out_shape=jax.ShapeDtypeStruct((LINES, LANE...  1.33 us
  transfers between devices with their start and end apart: 3, of which 2 were waited for; matrix products, arithmetic and copies ran while one was open for 0% of the time, Pallas kernels for 8%

profile of v2, /device:TPU:4, one launch (start us, length us, event | category | flops | bytes accessed | tf_op | source)
XLA Modules:
  0.0 43.3 jit_solution(2490879354146571752)
XLA Ops:
  0.0 0.0 copy-start.2
  0.0 0.0 copy-start
  0.0 0.0 copy-start.1
  0.0 1.3 %outlet.1 = f32[32,128]{1,0:T(8,128)S(1)} custom-call(f32[35,32,256]{2,1,0:T(8,128)} %bitcast.4, f32[5,7,32]{2,1,0:T(8,128)} %bitcast.9), custom_call_target="tpu_custom_call" | custom-call | flops 10000 | bytes 600000 | tf_op jit(solution)/shard_map/outlet/pallas_call | solution.py:79
  1.3 1.9 %collective-permute-start = (f32[32,128]{1,0:T(8,128)S(1)}, f32[32,128]{1,0:T(8,128)S(1)}, u32[]{:S(2)}, u32[]{:S(2)}) collective-permute-start(f32[32,128]{1,0:T(8,128)S(1)} %outlet.1), channel_id=1, source_target_pairs={{0,256},{1,257},{2,258},{3,259},{4,260},{5,261},{6,262},{7,263},{8... | collective-permute-start | bytes 49160 | tf_op jit(solution)/shard_map/ppermute | solution.py:467
  3.3 0.0 copy-done.2
  3.3 3.1 %collective-permute-done.mid = f32[32,128]{1,0:T(8,128)S(1)} collective-permute-done((f32[32,128]{1,0:T(8,128)S(1)}, f32[32,128]{1,0:T(8,128)S(1)}, u32[]{:S(2)}, u32[]{:S(2)}) %collective-permute-start) | collective-permute-done | bytes 16416 | tf_op jit(solution)/shard_map/ppermute | solution.py:467
  6.4 0.0 copy-done
  6.4 0.0 copy-done.1
  6.4 9.7 %early.1 = (f32[624,128]{1,0:T(8,128)S(1)}, f32[624,128]{1,0:T(8,128)S(1)}, f32[7,8,128]{2,1,0:T(8,128)S(1)}, f32[35,32,256]{2,1,0:T(8,128)}, f32[70,32,128]{2,1...) custom-call(s32[1,32]{1,0:T(1,128)} %pair_ref.3, ...), custom_call_target="tpu_custom_call" | custom-call | flops 30000000 | bytes 3000000 | tf_op jit(solution)/shard_map/early/pallas_call | solution.py:310
  16.1 1.9 %collective-permute-start.2 = (f32[624,128]{1,0:T(8,128)S(1)}, f32[624,128]{1,0:T(8,128)S(1)}, u32[]{:S(2)}, u32[]{:S(2)}) collective-permute-start(f32[624,128]{1,0:T(8,128)S(1)} %get-tuple-element.33), channel_id=1, source_target_pairs={{0,1},{1,2},{2,3},{3,4},{4,5},{5,6},{6,7},{7,8},{8,9},{9,10},{10,1... | collective-permute-start | bytes 958472 | tf_op jit(solution)/shard_map/ppermute | solution.py:471
  18.0 14.4 %collective-permute-start.1 = (f32[624,128]{1,0:T(8,128)S(1)}, f32[624,128]{1,0:T(8,128)S(1)}, u32[]{:S(2)}, u32[]{:S(2)}) collective-permute-start(f32[624,128]{1,0:T(8,128)S(1)} %get-tuple-element.20), channel_id=1, source_target_pairs={{1,0},{2,1},{3,2},{4,3},{5,4},{6,5},{7,6},{8,7},{9,8},{10,9},{11,1... | collective-permute-start | bytes 958472 | tf_op jit(solution)/shard_map/ppermute | solution.py:472
  32.5 0.8 %late.1 = (f32[35,32,256]{2,1,0:T(8,128)}, f32[70,32,128]{2,1,0:T(8,128)S(1)}, f32[50,32,128]{2,1,0:T(8,128)S(1)}, f32[35,32,128]{2,1,0:T(8,128)S(1)}, f32[70,32...) custom-call(s32[1,32]{1,0:T(1,128)} %pair_ref.3, f32[1,5,5]{2,1,0:T(8,128)S(1)} %copy.14.flux, ...), custom_call_target="tpu_custom_call", output_to_operand_aliasing={{0}: (7, {})} | custom-call | flops 30000000 | bytes 3000000 | tf_op jit(solution)/shard_map/late/pallas_call | solution.py:346
  33.2 4.4 %collective-permute-done.2.got = f32[624,128]{1,0:T(8,128)S(1)} collective-permute-done((f32[624,128]{1,0:T(8,128)S(1)}, f32[624,128]{1,0:T(8,128)S(1)}, u32[]{:S(2)}, u32[]{:S(2)}) %collective-permute-start.2) | collective-permute-done | bytes 319520 | tf_op jit(solution)/shard_map/ppermute | solution.py:471
  37.6 2.8 %high.1.rest_10_ = f32[35,32,256]{2,1,0:T(8,128)} custom-call(f32[1,5,5]{2,1,0:T(8,128)S(1)} %copy.14.flux, s32[4,3]{1,0:T(4,128)S(1)} %copy-done, f32[624,128]{1,0:T(8,128)S(1)} %collective-permute-done.2.got, f32[70,32,128]{2,1,0:T(8,128)S(1)} %get-tuple-element.21.rest_0_, ...), custom_call_target="tpu_custom_call", output_to_operand_aliasing={{}: (13, {})} | custom-call | flops 10000000 | bytes 1000000 | tf_op jit(solution)/shard_map/high/pallas_call | solution.py:426
  40.5 0.0 collective-permute-done.1.got
  40.5 2.8 %low.1 = f32[35,32,256]{2,1,0:T(8,128)} custom-call(f32[1,5,5]{2,1,0:T(8,128)S(1)} %copy.14.flux, s32[4,3]{1,0:T(4,128)S(1)} %copy-done, f32[624,128]{1,0:T(8,128)S(1)} %collective-permute-done.1.got, f32[70,32,128]{2,1,0:T(8,128)S(1)} %get-tuple-element.21.rest_0_, f32[50,32,128]{2,1,0:T(8,128)S(1)} %get-tuple-element.22.rest_1_, ...), custom_call_target="tpu_custom_call", output_to_operand_aliasing={{}: (13, {})} | custom-call | flops 10000000 | bytes 1000000 | tf_op jit(solution)/shard_map/low/pallas_call | solution.py:426
  (1 shorter events, 0.0 us)
Async XLA Ops:
  0.0 3.3 %copy-start.2 = (f32[1,5,5]{2,0,1:T(1,128)S(1)}, f32[1,5,5]{2,0,1:T(1,128)}, u32[]{:S(2)}) copy-start(f32[1,5,5]{2,0,1:T(1,128)} %param.9) | copy-start | bytes 304
  0.0 6.4 %copy-start = (s32[4,3]{1,0:T(4,128)S(1)}, s32[4,3]{1,0:T(4,128)}, u32[]{:S(2)}) copy-start(s32[4,3]{1,0:T(4,128)} %modes_ref.7) | copy-start | bytes 148
  0.0 6.4 %copy-start.1 = (f32[4]{0:T(128)S(1)}, f32[4]{0:T(128)}, u32[]{:S(2)}) copy-start(f32[4]{0:T(128)} %delay_ref.1) | copy-start | bytes 52
  1.3 5.1 %collective-permute-start = (f32[32,128]{1,0:T(8,128)S(1)}, f32[32,128]{1,0:T(8,128)S(1)}, u32[]{:S(2)}, u32[]{:S(2)}) collective-permute-start(f32[32,128]{1,0:T(8,128)S(1)} %outlet.1), channel_id=1, source_target_pairs={{0,256},{1,257},{2,258},{3,259},{4,260},{5,261},{6,262},{7,263},{8... | collective-permute-start | bytes 49160 | tf_op jit(solution)/shard_map/ppermute | solution.py:467
  16.1 21.5 %collective-permute-start.2 = (f32[624,128]{1,0:T(8,128)S(1)}, f32[624,128]{1,0:T(8,128)S(1)}, u32[]{:S(2)}, u32[]{:S(2)}) collective-permute-start(f32[624,128]{1,0:T(8,128)S(1)} %get-tuple-element.33), channel_id=1, source_target_pairs={{0,1},{1,2},{2,3},{3,4},{4,5},{5,6},{6,7},{7,8},{8,9},{9,10},{10,1... | collective-permute-start | bytes 958472 | tf_op jit(solution)/shard_map/ppermute | solution.py:471
  18.0 22.4 %collective-permute-start.1 = (f32[624,128]{1,0:T(8,128)S(1)}, f32[624,128]{1,0:T(8,128)S(1)}, u32[]{:S(2)}, u32[]{:S(2)}) collective-permute-start(f32[624,128]{1,0:T(8,128)S(1)} %get-tuple-element.20), channel_id=1, source_target_pairs={{1,0},{2,1},{3,2},{4,3},{5,4},{6,5},{7,6},{8,7},{9,8},{10,9},{11,1... | collective-permute-start | bytes 958472 | tf_op jit(solution)/shard_map/ppermute | solution.py:472
